TPU v7x, 32 devices: a whole 2x2x4 slice. The times are simulated.
32 devices in a mesh: gx: 16 (over z, x, core), gy: 2 (over y).
Axes of the slice: x: 2, y: 2, z: 4, core: 2. Of those that a mesh axis runs over, the one named last changes fastest.
Arguments:
- residual: float32 [4, 3, 16, 128, 512], P(None, None, None, 'gx', 'gy'), may hold values from -6 to 6
- eps_inv: float32 [16, 128, 512], P(None, 'gx', 'gy'), may hold values from 0.08 to 1
- region_ids: int32 [16, 128, 512], P(None, 'gx', 'gy'), may hold values from 0 to 7
- source_mask: int32 [16, 128, 512], P(None, 'gx', 'gy'), may hold values 0 or 1
- pole_a: float32 [8, 2], replicated, may hold values from 1.2 to 1.9602, as said below
- pole_b: float32 [8, 2], replicated, may hold values from -0.98 to -0.8
- pole_c: float32 [8, 2], replicated, may hold values from 0.1 to 0.4
- waveform: float32 [64, 4], replicated, may hold values from -4 to 4
- plan: int32 [4], replicated, may hold values from 0 to 63
Outputs:
- adjoint_e: float32 [4, 3, 16, 128, 512], P(None, None, None, 'gx', 'gy')
- adjoint_h: float32 [4, 3, 16, 128, 512], P(None, None, None, 'gx', 'gy')
Inputs may be any that keep to these rules, and one draw needn't show every extreme that they name: For each region and pole, pole_a is at least 1.2 and below 0.99 * (1 - pole_b), so each pole's recurrence is stable.
All inputs are finite; a program needn't handle non-finite values. No bound on the sum of `source_mask` on one device may be relied on, other than what follows from the above.
Results may differ from a plain program's by a relative error of at most 0.00002.
Values sent between devices are 32-bit elements; how exact they have to be, the bound alone decides.
No kernel may reach another device: no remote copies, remote signals or barrier semaphores. Data moves between devices by JAX's collectives and lax.ppermute only.
A program may use at most 64 MiB of HBM per device.

v0:
```python
import jax
import jax.numpy as jnp
from jax import lax
from jax.sharding import PartitionSpec as P

STEPS = 4


def from_behind(value, axis, steps):
    count = lax.axis_size(axis)
    initial, last = (max(0, -steps), min(count, count - steps))
    return lax.ppermute(value, axis, [(source, source + steps) for source in range(initial, last)])


def upper_cell(field, axis):
    count = field.shape[axis]
    inner = lax.slice_in_dim(field, 1, count, axis=axis)
    zeros = jnp.zeros_like(lax.slice_in_dim(field, 0, 1, axis=axis))
    return jnp.concatenate([inner, zeros], axis)


def lower_cell(field, axis):
    count = field.shape[axis]
    inner = lax.slice_in_dim(field, 0, count - 1, axis=axis)
    zeros = jnp.zeros_like(lax.slice_in_dim(field, 0, 1, axis=axis))
    return jnp.concatenate([zeros, inner], axis)


def region_lookup(region_ids, table, pole):
    value = jnp.zeros(region_ids.shape, jnp.float32)
    for region in range(table.shape[0]):
        value = jnp.where(region_ids == region, table[region, pole], value)
    return value


def electric_next(elec):
    elec_x, elec_y, elec_z = elec
    x_faces = from_behind((elec_y[:, :, 0:1, :], elec_z[:, :, 0:1, :]), "gx", -1)
    y_faces = from_behind((elec_x[:, :, :, 0:1], elec_z[:, :, :, 0:1]), "gy", -1)
    return (
        jnp.concatenate([elec_y[:, :, 1:, :], x_faces[0]], 2),
        jnp.concatenate([elec_z[:, :, 1:, :], x_faces[1]], 2),
        jnp.concatenate([elec_x[:, :, :, 1:], y_faces[0]], 3),
        jnp.concatenate([elec_z[:, :, :, 1:], y_faces[1]], 3),
    )


def magnetic_prev(magn):
    magn_x, magn_y, magn_z = magn
    last_x = magn_y.shape[2] - 1
    last_y = magn_x.shape[3] - 1
    x_faces = from_behind((magn_y[:, :, last_x:, :], magn_z[:, :, last_x:, :]), "gx", 1)
    y_faces = from_behind((magn_x[:, :, :, last_y:], magn_z[:, :, :, last_y:]), "gy", 1)
    return (
        jnp.concatenate([x_faces[0], magn_y[:, :, :last_x, :]], 2),
        jnp.concatenate([x_faces[1], magn_z[:, :, :last_x, :]], 2),
        jnp.concatenate([y_faces[0], magn_x[:, :, :, :last_y]], 3),
        jnp.concatenate([y_faces[1], magn_z[:, :, :, :last_y]], 3),
    )


def run_steps(
    residual, eps_cells, mask_float, region_ids, tables, waveform, plan, next_fn, prev_fn
):
    stored = [
        [region_lookup(region_ids, table, pole)[None] for table in tables] for pole in range(2)
    ]
    zeros = jnp.zeros(residual[:, 0].shape, jnp.float32)
    elec = [zeros, zeros, zeros]
    magn = [zeros, zeros, zeros]
    state_u = [[zeros, zeros, zeros], [zeros, zeros, zeros]]
    state_v = [[zeros, zeros, zeros], [zeros, zeros, zeros]]
    samples = jnp.arange(waveform.shape[0], dtype=jnp.int32)[:, None]
    for index_step in range(STEPS):
        amplitude = jnp.sum(jnp.where(samples == plan[index_step], waveform, 0.0), 0)
        scaled = amplitude[:, None, None, None]
        elec = [elec[c] + mask_float * residual[:, c] * scaled for c in range(3)]
        elec_x, elec_y, elec_z = elec
        ey_xnext, ez_xnext, ex_ynext, ez_ynext = next_fn(elec)
        curl_x = ez_ynext - elec_z - (upper_cell(elec_y, 1) - elec_y)
        curl_y = upper_cell(elec_x, 1) - elec_x - (ez_xnext - elec_z)
        curl_z = ey_xnext - elec_y - (ex_ynext - elec_x)
        magn = [magn[0] - 0.5 * curl_x, magn[1] - 0.5 * curl_y, magn[2] - 0.5 * curl_z]
        magn_x, magn_y, magn_z = magn
        hy_xprev, hz_xprev, hx_yprev, hz_yprev = prev_fn(magn)
        back_x = magn_z - hz_yprev - (magn_y - lower_cell(magn_y, 1))
        back_y = magn_x - lower_cell(magn_x, 1) - (magn_z - hz_xprev)
        back_z = magn_y - hy_xprev - (magn_x - hx_yprev)
        backs = [back_x, back_y, back_z]
        sectioned = [elec[c] + 0.5 * eps_cells * backs[c] for c in range(3)]
        change = [zeros, zeros, zeros]
        for pole in range(2):
            coef_a, coef_b, coef_c = stored[pole]
            new_u = [
                coef_a * state_u[pole][c] + state_v[pole][c] + coef_c * sectioned[c]
                for c in range(3)
            ]
            state_v[pole] = [coef_b * state_u[pole][c] for c in range(3)]
            change = [change[c] + (new_u[c] - state_u[pole][c]) for c in range(3)]
            state_u[pole] = new_u
        elec = [sectioned[c] - eps_cells * change[c] for c in range(3)]
    return (jnp.stack(elec, 1), jnp.stack(magn, 1))


def local(residual, eps_inv, region_ids, source_mask, pole_a, pole_b, pole_c, waveform, plan):
    tables = (pole_a, pole_b, pole_c)
    mask_float = source_mask.astype(jnp.float32)[None]
    eps_cells = eps_inv[None]
    return run_steps(
        residual,
        eps_cells,
        mask_float,
        region_ids,
        tables,
        waveform,
        plan,
        electric_next,
        magnetic_prev,
    )


def solution(mesh):
    placed = (
        P(None, None, None, "gx", "gy"),
        P(None, "gx", "gy"),
        P(None, "gx", "gy"),
        P(None, "gx", "gy"),
        P(),
        P(),
        P(),
        P(),
        P(),
    )
    return jax.shard_map(
        local,
        mesh=mesh,
        in_specs=placed,
        out_specs=(P(None, None, None, "gx", "gy"), P(None, None, None, "gx", "gy")),
        check_vma=False,
    )
```

profile of v0, /device:TPU:6, one launch (start us, length us, event | category | flops | bytes accessed | tf_op | source)
XLA Modules:
  0.0 173.7 jit_solution(4274038090405800252)
XLA Ops:
  8.2 1.9 %collective-permute-start.3 = (f32[4,16,1,256]{3,2,1,0:T(1,128)S(1)}, f32[4,16,1,256]{3,2,1,0:T(1,128)S(1)}, u32[]{:S(2)}, u32[]{:S(2)}) collective-permute-start(f32[4,16,1,256]{3,2,1,0:T(1,128)S(1)} %slice.557), channel_id=1, source_target_pairs={{2,0},{4,2},{6,4},{8,6},{10,8},{12,10},{14,12},{16,14},{18,16},{20... | collective-permute-start | bytes 196616 | tf_op jit(solution)/shard_map/ppermute | solution.py:12
  10.2 2.5 %collective-permute-start = (f32[4,16,1,256]{3,2,1,0:T(1,128)S(1)}, f32[4,16,1,256]{3,2,1,0:T(1,128)S(1)}, u32[]{:S(2)}, u32[]{:S(2)}) collective-permute-start(f32[4,16,1,256]{3,2,1,0:T(1,128)S(1)} %slice.550), channel_id=1, source_target_pairs={{2,0},{4,2},{6,4},{8,6},{10,8},{12,10},{14,12},{16,14},{18,16},{20... | collective-permute-start | bytes 196616 | tf_op jit(solution)/shard_map/ppermute | solution.py:12
  18.1 5.2 %broadcast_multiply_fusion.1 = (f32[16,8,256]{2,1,0:T(8,128)S(1)}, f32[16,8,256]{2,1,0:T(8,128)S(1)}, pred[16,8,256]{2,1,0:T(8,128)(4,1)S(1)}, pred[16,8,256]{2,...) fusion(f32[]{:T(128)} %bitcast.44, f32[]{:T(128)} %bitcast.43, ...), kind=kLoop, calls=%fused_computation.155 | loop fusion | flops 557056 | bytes 655392 | tf_op jit(solution)/shard_map/mul | solution.py:98
  23.2 5.1 %broadcast_multiply_fusion.2 = (f32[16,8,256]{2,1,0:T(8,128)S(1)}, f32[16,8,256]{2,1,0:T(8,128)S(1)}) fusion(pred[16,8,256]{2,1,0:T(8,128)(4,1)S(1)} %get-tuple-element.23, pred[16,8,256]{2,1,0:T(8,128)(4,1)S(1)} %get-tuple-element.22, pred[16,8,256]{2,1,0:T(8,128)(4,1)S(1)} %get-tuple-element.21, pred[16,8,256]{2,1,0:T(8,128)(4,1)S(1)} %get-tuple-element.20, ...), kind=kLoop, calls=%fused_computation.156 | loop fusion | flops 294912 | bytes 524320 | tf_op jit(solution)/shard_map/mul | solution.py:95
  28.3 5.0 %select_select_fusion.2 = (f32[16,8,256]{2,1,0:T(8,128)S(1)}, f32[16,8,256]{2,1,0:T(8,128)S(1)}) fusion(pred[16,8,256]{2,1,0:T(8,128)(4,1)S(1)} %get-tuple-element.23, pred[16,8,256]{2,1,0:T(8,128)(4,1)S(1)} %get-tuple-element.22, pred[16,8,256]{2,1,0:T(8,128)(4,1)S(1)} %get-tuple-element.21, pred[16,8,256]{2,1,0:T(8,128)(4,1)S(1)} %get-tuple-element.20, ...), kind=kLoop, calls=%fused_computation.150 | loop fusion | flops 294912 | bytes 655392 | tf_op jit(solution)/shard_map/jit(_where)/select_n | solution.py:32
  33.3 5.1 %broadcast_multiply_fusion.3 = (f32[16,8,256]{2,1,0:T(8,128)S(1)}, f32[16,8,256]{2,1,0:T(8,128)S(1)}) fusion(pred[16,8,256]{2,1,0:T(8,128)(4,1)S(1)} %get-tuple-element.23, pred[16,8,256]{2,1,0:T(8,128)(4,1)S(1)} %get-tuple-element.22, pred[16,8,256]{2,1,0:T(8,128)(4,1)S(1)} %get-tuple-element.21, pred[16,8,256]{2,1,0:T(8,128)(4,1)S(1)} %get-tuple-element.20, ...), kind=kLoop, calls=%fused_computation.157 | loop fusion | flops 294912 | bytes 524320 | tf_op jit(solution)/shard_map/mul | solution.py:95
  39.7 2.1 %collective-permute-start.9 = (f32[4,16,1,256]{3,2,1,0:T(1,128)S(1)}, f32[4,16,1,256]{3,2,1,0:T(1,128)S(1)}, u32[]{:S(2)}, u32[]{:S(2)}) collective-permute-start(f32[4,16,1,256]{3,2,1,0:T(1,128)S(1)} %slice.572), channel_id=1, source_target_pairs={{0,2},{2,4},{4,6},{6,8},{8,10},{10,12},{12,14},{14,16},{16,18},{18... | collective-permute-start | bytes 196616 | tf_op jit(solution)/shard_map/ppermute | solution.py:12
  43.5 5.1 %select_select_fusion.4 = f32[16,8,256]{2,1,0:T(8,128)S(1)} fusion(pred[16,8,256]{2,1,0:T(8,128)(4,1)S(1)} %get-tuple-element.23, pred[16,8,256]{2,1,0:T(8,128)(4,1)S(1)} %get-tuple-element.22, pred[16,8,256]{2,1,0:T(8,128)(4,1)S(1)} %get-tuple-element.21, pred[16,8,256]{2,1,0:T(8,128)(4,1)S(1)} %get-tuple-element.20, ...), kind=kLoop, calls=%fused_computation.152 | loop fusion | flops 262144 | bytes 393248 | tf_op jit(solution)/shard_map/jit(_where)/select_n | solution.py:32
  48.8 4.8 %collective-permute-start.5 = (f32[4,16,1,256]{3,2,1,0:T(1,128)S(1)}, f32[4,16,1,256]{3,2,1,0:T(1,128)S(1)}, u32[]{:S(2)}, u32[]{:S(2)}) collective-permute-start(f32[4,16,1,256]{3,2,1,0:T(1,128)S(1)} %slice.563), channel_id=1, source_target_pairs={{0,2},{2,4},{4,6},{6,8},{8,10},{10,12},{12,14},{14,16},{16,18},{18... | collective-permute-start | bytes 196616 | tf_op jit(solution)/shard_map/ppermute | solution.py:12
  59.8 4.3 %collective-permute-done.2 = f32[4,16,8,1]{3,2,1,0:T(8,128)S(1)} collective-permute-done((f32[4,16,8,1]{3,2,1,0:T(8,128)S(1)}, f32[4,16,8,1]{3,2,1,0:T(8,128)S(1)}, u32[]{:S(2)}, u32[]{:S(2)}) %collective-permute-start.2) | collective-permute-done | bytes 2080 | tf_op jit(solution)/shard_map/ppermute | solution.py:12
  67.9 4.7 %collective-permute-done.7 = f32[4,16,8,1]{3,2,1,0:T(8,128)S(1)} collective-permute-done((f32[4,16,8,1]{3,2,1,0:T(8,128)S(1)}, f32[4,16,8,1]{3,2,1,0:T(8,128)S(1)}, u32[]{:S(2)}, u32[]{:S(2)}) %collective-permute-start.7) | collective-permute-done | bytes 2080 | tf_op jit(solution)/shard_map/ppermute | solution.py:12
  72.6 4.2 %collective-permute-done.12 = f32[4,16,8,1]{3,2,1,0:T(8,128)S(1)} collective-permute-done((f32[4,16,8,1]{3,2,1,0:T(8,128)S(1)}, f32[4,16,8,1]{3,2,1,0:T(8,128)S(1)}, u32[]{:S(2)}, u32[]{:S(2)}) %collective-permute-start.12) | collective-permute-done | bytes 2080 | tf_op jit(solution)/shard_map/ppermute | solution.py:12
  80.9 5.1 %broadcast_multiply_fusion = (f32[16,8,256]{2,1,0:T(8,128)S(1)}, f32[16,8,256]{2,1,0:T(8,128)S(1)}) fusion(pred[16,8,256]{2,1,0:T(8,128)(4,1)S(1)} %get-tuple-element.23, pred[16,8,256]{2,1,0:T(8,128)(4,1)S(1)} %get-tuple-element.22, pred[16,8,256]{2,1,0:T(8,128)(4,1)S(1)} %get-tuple-element.21, pred[16,8,256]{2,1,0:T(8,128)(4,1)S(1)} %get-tuple-element.20, ...), kind=kLoop, calls=%fused_computation.154 | loop fusion | flops 294912 | bytes 524320 | tf_op jit(solution)/shard_map/mul | solution.py:98
  86.3 4.3 %collective-permute-start.13 = (f32[4,16,1,256]{3,2,1,0:T(1,128)S(1)}, f32[4,16,1,256]{3,2,1,0:T(1,128)S(1)}, u32[]{:S(2)}, u32[]{:S(2)}) collective-permute-start(f32[4,16,1,256]{3,2,1,0:T(1,128)S(1)} %slice.583), channel_id=1, source_target_pairs={{0,2},{2,4},{4,6},{6,8},{8,10},{10,12},{12,14},{14,16},{16,18},{18... | collective-permute-start | bytes 196616 | tf_op jit(solution)/shard_map/ppermute | solution.py:12
  97.2 3.9 %collective-permute-done.8 = f32[4,16,8,1]{3,2,1,0:T(8,128)S(1)} collective-permute-done((f32[4,16,8,1]{3,2,1,0:T(8,128)S(1)}, f32[4,16,8,1]{3,2,1,0:T(8,128)S(1)}, u32[]{:S(2)}, u32[]{:S(2)}) %collective-permute-start.8) | collective-permute-done | bytes 2080 | tf_op jit(solution)/shard_map/ppermute | solution.py:12
  105.1 4.7 %collective-permute-done.15 = f32[4,16,8,1]{3,2,1,0:T(8,128)S(1)} collective-permute-done((f32[4,16,8,1]{3,2,1,0:T(8,128)S(1)}, f32[4,16,8,1]{3,2,1,0:T(8,128)S(1)}, u32[]{:S(2)}, u32[]{:S(2)}) %collective-permute-start.15) | collective-permute-done | bytes 2080 | tf_op jit(solution)/shard_map/ppermute | solution.py:12
  109.8 4.4 %collective-permute-done.20 = f32[4,16,8,1]{3,2,1,0:T(8,128)S(1)} collective-permute-done((f32[4,16,8,1]{3,2,1,0:T(8,128)S(1)}, f32[4,16,8,1]{3,2,1,0:T(8,128)S(1)}, u32[]{:S(2)}, u32[]{:S(2)}) %collective-permute-start.20) | collective-permute-done | bytes 2080 | tf_op jit(solution)/shard_map/ppermute | solution.py:12
  118.5 4.6 %collective-permute-start.21 = (f32[4,16,1,256]{3,2,1,0:T(1,128)S(1)}, f32[4,16,1,256]{3,2,1,0:T(1,128)S(1)}, u32[]{:S(2)}, u32[]{:S(2)}) collective-permute-start(f32[4,16,1,256]{3,2,1,0:T(1,128)S(1)} %slice.603), channel_id=1, source_target_pairs={{0,2},{2,4},{4,6},{6,8},{8,10},{10,12},{12,14},{14,16},{16,18},{18... | collective-permute-start | bytes 196616 | tf_op jit(solution)/shard_map/ppermute | solution.py:12
  127.1 2.2 %collective-permute-start.27 = (f32[4,16,1,256]{3,2,1,0:T(1,128)S(1)}, f32[4,16,1,256]{3,2,1,0:T(1,128)S(1)}, u32[]{:S(2)}, u32[]{:S(2)}) collective-permute-start(f32[4,16,1,256]{3,2,1,0:T(1,128)S(1)} %slice.617), channel_id=1, source_target_pairs={{2,0},{4,2},{6,4},{8,6},{10,8},{12,10},{14,12},{16,14},{18,16},{20... | collective-permute-start | bytes 196616 | tf_op jit(solution)/shard_map/ppermute | solution.py:12
  137.8 4.7 %collective-permute-done.23 = f32[4,16,8,1]{3,2,1,0:T(8,128)S(1)} collective-permute-done((f32[4,16,8,1]{3,2,1,0:T(8,128)S(1)}, f32[4,16,8,1]{3,2,1,0:T(8,128)S(1)}, u32[]{:S(2)}, u32[]{:S(2)}) %collective-permute-start.23) | collective-permute-done | bytes 2080 | tf_op jit(solution)/shard_map/ppermute | solution.py:12
  142.6 4.7 %collective-permute-done.28 = f32[4,16,8,1]{3,2,1,0:T(8,128)S(1)} collective-permute-done((f32[4,16,8,1]{3,2,1,0:T(8,128)S(1)}, f32[4,16,8,1]{3,2,1,0:T(8,128)S(1)}, u32[]{:S(2)}, u32[]{:S(2)}) %collective-permute-start.28) | collective-permute-done | bytes 2080 | tf_op jit(solution)/shard_map/ppermute | solution.py:12
  150.2 5.0 %collective-permute-start.30 = (f32[4,16,1,256]{3,2,1,0:T(1,128)S(1)}, f32[4,16,1,256]{3,2,1,0:T(1,128)S(1)}, u32[]{:S(2)}, u32[]{:S(2)}) collective-permute-start(f32[4,16,1,256]{3,2,1,0:T(1,128)S(1)} %slice.625), channel_id=1, source_target_pairs={{0,2},{2,4},{4,6},{6,8},{8,10},{10,12},{12,14},{14,16},{16,18},{18... | collective-permute-start | bytes 196616 | tf_op jit(solution)/shard_map/ppermute | solution.py:12
  159.2 7.1 %collective-permute-done.24 = f32[4,16,8,1]{3,2,1,0:T(8,128)S(1)} collective-permute-done((f32[4,16,8,1]{3,2,1,0:T(8,128)S(1)}, f32[4,16,8,1]{3,2,1,0:T(8,128)S(1)}, u32[]{:S(2)}, u32[]{:S(2)}) %collective-permute-start.24) | collective-permute-done | bytes 2080 | tf_op jit(solution)/shard_map/ppermute | solution.py:12
  168.4 2.8 %collective-permute-done.31 = f32[4,16,8,1]{3,2,1,0:T(8,128)S(1)} collective-permute-done((f32[4,16,8,1]{3,2,1,0:T(8,128)S(1)}, f32[4,16,8,1]{3,2,1,0:T(8,128)S(1)}, u32[]{:S(2)}, u32[]{:S(2)}) %collective-permute-start.31) | collective-permute-done | bytes 2080 | tf_op jit(solution)/shard_map/ppermute | solution.py:12
  (160 shorter events, 68.3 us)
Async XLA Ops:
  8.2 30.9 %collective-permute-start.3 = (f32[4,16,1,256]{3,2,1,0:T(1,128)S(1)}, f32[4,16,1,256]{3,2,1,0:T(1,128)S(1)}, u32[]{:S(2)}, u32[]{:S(2)}) collective-permute-start(f32[4,16,1,256]{3,2,1,0:T(1,128)S(1)} %slice.557), channel_id=1, source_target_pairs={{2,0},{4,2},{6,4},{8,6},{10,8},{12,10},{14,12},{16,14},{18,16},{20... | collective-permute-start | bytes 196616 | tf_op jit(solution)/shard_map/ppermute | solution.py:12
  10.2 28.9 %collective-permute-start = (f32[4,16,1,256]{3,2,1,0:T(1,128)S(1)}, f32[4,16,1,256]{3,2,1,0:T(1,128)S(1)}, u32[]{:S(2)}, u32[]{:S(2)}) collective-permute-start(f32[4,16,1,256]{3,2,1,0:T(1,128)S(1)} %slice.550), channel_id=1, source_target_pairs={{2,0},{4,2},{6,4},{8,6},{10,8},{12,10},{14,12},{16,14},{18,16},{20... | collective-permute-start | bytes 196616 | tf_op jit(solution)/shard_map/ppermute | solution.py:12
  12.7 26.3 %collective-permute-start.4 = (f32[4,16,8,1]{3,2,1,0:T(8,128)S(1)}, f32[4,16,8,1]{3,2,1,0:T(8,128)S(1)}, u32[]{:S(2)}, u32[]{:S(2)}) collective-permute-start(f32[4,16,8,1]{3,2,1,0:T(8,128)S(1)} %slice.560), channel_id=1, source_target_pairs={{1,0},{3,2},{5,4},{7,6},{9,8},{11,10},{13,12},{15,14},{17,16},{19,... | collective-permute-start | bytes 6152 | tf_op jit(solution)/shard_map/ppermute | solution.py:12
  14.6 24.5 %collective-permute-start.1 = (f32[4,16,8,1]{3,2,1,0:T(8,128)S(1)}, f32[4,16,8,1]{3,2,1,0:T(8,128)S(1)}, u32[]{:S(2)}, u32[]{:S(2)}) collective-permute-start(f32[4,16,8,1]{3,2,1,0:T(8,128)S(1)} %slice.552), channel_id=1, source_target_pairs={{1,0},{3,2},{5,4},{7,6},{9,8},{11,10},{13,12},{15,14},{17,16},{19,... | collective-permute-start | bytes 6152 | tf_op jit(solution)/shard_map/ppermute | solution.py:12
  39.7 15.2 %collective-permute-start.9 = (f32[4,16,1,256]{3,2,1,0:T(1,128)S(1)}, f32[4,16,1,256]{3,2,1,0:T(1,128)S(1)}, u32[]{:S(2)}, u32[]{:S(2)}) collective-permute-start(f32[4,16,1,256]{3,2,1,0:T(1,128)S(1)} %slice.572), channel_id=1, source_target_pairs={{0,2},{2,4},{4,6},{6,8},{8,10},{10,12},{12,14},{14,16},{16,18},{18... | collective-permute-start | bytes 196616 | tf_op jit(solution)/shard_map/ppermute | solution.py:12
  42.0 12.9 %collective-permute-start.10 = (f32[4,16,8,1]{3,2,1,0:T(8,128)S(1)}, f32[4,16,8,1]{3,2,1,0:T(8,128)S(1)}, u32[]{:S(2)}, u32[]{:S(2)}) collective-permute-start(f32[4,16,8,1]{3,2,1,0:T(8,128)S(1)} %slice.574), channel_id=1, source_target_pairs={{0,1},{2,3},{4,5},{6,7},{8,9},{10,11},{12,13},{14,15},{16,17},{18,... | collective-permute-start | bytes 6152 | tf_op jit(solution)/shard_map/ppermute | solution.py:12
  55.5 21.4 %collective-permute-start.11 = (f32[4,16,1,256]{3,2,1,0:T(1,128)S(1)}, f32[4,16,1,256]{3,2,1,0:T(1,128)S(1)}, u32[]{:S(2)}, u32[]{:S(2)}) collective-permute-start(f32[4,16,1,256]{3,2,1,0:T(1,128)S(1)} %slice.577), channel_id=1, source_target_pairs={{2,0},{4,2},{6,4},{8,6},{10,8},{12,10},{14,12},{16,14},{18,16},{20... | collective-permute-start | bytes 196616 | tf_op jit(solution)/shard_map/ppermute | solution.py:12
  57.9 19.0 %collective-permute-start.6 = (f32[4,16,1,256]{3,2,1,0:T(1,128)S(1)}, f32[4,16,1,256]{3,2,1,0:T(1,128)S(1)}, u32[]{:S(2)}, u32[]{:S(2)}) collective-permute-start(f32[4,16,1,256]{3,2,1,0:T(1,128)S(1)} %slice.566), channel_id=1, source_target_pairs={{2,0},{4,2},{6,4},{8,6},{10,8},{12,10},{14,12},{16,14},{18,16},{20... | collective-permute-start | bytes 196616 | tf_op jit(solution)/shard_map/ppermute | solution.py:12
  66.0 10.9 %collective-permute-start.12 = (f32[4,16,8,1]{3,2,1,0:T(8,128)S(1)}, f32[4,16,8,1]{3,2,1,0:T(8,128)S(1)}, u32[]{:S(2)}, u32[]{:S(2)}) collective-permute-start(f32[4,16,8,1]{3,2,1,0:T(8,128)S(1)} %slice.580), channel_id=1, source_target_pairs={{1,0},{3,2},{5,4},{7,6},{9,8},{11,10},{13,12},{15,14},{17,16},{19,... | collective-permute-start | bytes 6152 | tf_op jit(solution)/shard_map/ppermute | solution.py:12
  77.6 14.4 %collective-permute-start.17 = (f32[4,16,1,256]{3,2,1,0:T(1,128)S(1)}, f32[4,16,1,256]{3,2,1,0:T(1,128)S(1)}, u32[]{:S(2)}, u32[]{:S(2)}) collective-permute-start(f32[4,16,1,256]{3,2,1,0:T(1,128)S(1)} %slice.592), channel_id=1, source_target_pairs={{0,2},{2,4},{4,6},{6,8},{8,10},{10,12},{12,14},{14,16},{16,18},{18... | collective-permute-start | bytes 196616 | tf_op jit(solution)/shard_map/ppermute | solution.py:12
  79.6 12.4 %collective-permute-start.18 = (f32[4,16,8,1]{3,2,1,0:T(8,128)S(1)}, f32[4,16,8,1]{3,2,1,0:T(8,128)S(1)}, u32[]{:S(2)}, u32[]{:S(2)}) collective-permute-start(f32[4,16,8,1]{3,2,1,0:T(8,128)S(1)} %slice.594), channel_id=1, source_target_pairs={{0,1},{2,3},{4,5},{6,7},{8,9},{10,11},{12,13},{14,15},{16,17},{18,... | collective-permute-start | bytes 6152 | tf_op jit(solution)/shard_map/ppermute | solution.py:12
  92.7 21.5 %collective-permute-start.19 = (f32[4,16,1,256]{3,2,1,0:T(1,128)S(1)}, f32[4,16,1,256]{3,2,1,0:T(1,128)S(1)}, u32[]{:S(2)}, u32[]{:S(2)}) collective-permute-start(f32[4,16,1,256]{3,2,1,0:T(1,128)S(1)} %slice.597), channel_id=1, source_target_pairs={{2,0},{4,2},{6,4},{8,6},{10,8},{12,10},{14,12},{16,14},{18,16},{20... | collective-permute-start | bytes 196616 | tf_op jit(solution)/shard_map/ppermute | solution.py:12
  95.3 19.0 %collective-permute-start.14 = (f32[4,16,1,256]{3,2,1,0:T(1,128)S(1)}, f32[4,16,1,256]{3,2,1,0:T(1,128)S(1)}, u32[]{:S(2)}, u32[]{:S(2)}) collective-permute-start(f32[4,16,1,256]{3,2,1,0:T(1,128)S(1)} %slice.586), channel_id=1, source_target_pairs={{2,0},{4,2},{6,4},{8,6},{10,8},{12,10},{14,12},{16,14},{18,16},{20... | collective-permute-start | bytes 196616 | tf_op jit(solution)/shard_map/ppermute | solution.py:12
  103.2 11.0 %collective-permute-start.20 = (f32[4,16,8,1]{3,2,1,0:T(8,128)S(1)}, f32[4,16,8,1]{3,2,1,0:T(8,128)S(1)}, u32[]{:S(2)}, u32[]{:S(2)}) collective-permute-start(f32[4,16,8,1]{3,2,1,0:T(8,128)S(1)} %slice.600), channel_id=1, source_target_pairs={{1,0},{3,2},{5,4},{7,6},{9,8},{11,10},{13,12},{15,14},{17,16},{19,... | collective-permute-start | bytes 6152 | tf_op jit(solution)/shard_map/ppermute | solution.py:12
  114.9 11.3 %collective-permute-start.25 = (f32[4,16,1,256]{3,2,1,0:T(1,128)S(1)}, f32[4,16,1,256]{3,2,1,0:T(1,128)S(1)}, u32[]{:S(2)}, u32[]{:S(2)}) collective-permute-start(f32[4,16,1,256]{3,2,1,0:T(1,128)S(1)} %slice.612), channel_id=1, source_target_pairs={{0,2},{2,4},{4,6},{6,8},{8,10},{10,12},{12,14},{14,16},{16,18},{18... | collective-permute-start | bytes 196616 | tf_op jit(solution)/shard_map/ppermute | solution.py:12
  118.5 10.8 %collective-permute-start.21 = (f32[4,16,1,256]{3,2,1,0:T(1,128)S(1)}, f32[4,16,1,256]{3,2,1,0:T(1,128)S(1)}, u32[]{:S(2)}, u32[]{:S(2)}) collective-permute-start(f32[4,16,1,256]{3,2,1,0:T(1,128)S(1)} %slice.603), channel_id=1, source_target_pairs={{0,2},{2,4},{4,6},{6,8},{8,10},{10,12},{12,14},{14,16},{16,18},{18... | collective-permute-start | bytes 196616 | tf_op jit(solution)/shard_map/ppermute | solution.py:12
  123.1 10.5 %collective-permute-start.16 = (f32[4,16,8,1]{3,2,1,0:T(8,128)S(1)}, f32[4,16,8,1]{3,2,1,0:T(8,128)S(1)}, u32[]{:S(2)}, u32[]{:S(2)}) collective-permute-start(f32[4,16,8,1]{3,2,1,0:T(8,128)S(1)} %slice.589), channel_id=1, source_target_pairs={{0,1},{2,3},{4,5},{6,7},{8,9},{10,11},{12,13},{14,15},{16,17},{18,... | collective-permute-start | bytes 6152 | tf_op jit(solution)/shard_map/ppermute | solution.py:12
  127.1 20.2 %collective-permute-start.27 = (f32[4,16,1,256]{3,2,1,0:T(1,128)S(1)}, f32[4,16,1,256]{3,2,1,0:T(1,128)S(1)}, u32[]{:S(2)}, u32[]{:S(2)}) collective-permute-start(f32[4,16,1,256]{3,2,1,0:T(1,128)S(1)} %slice.617), channel_id=1, source_target_pairs={{2,0},{4,2},{6,4},{8,6},{10,8},{12,10},{14,12},{16,14},{18,16},{20... | collective-permute-start | bytes 196616 | tf_op jit(solution)/shard_map/ppermute | solution.py:12
  130.1 17.2 %collective-permute-start.22 = (f32[4,16,1,256]{3,2,1,0:T(1,128)S(1)}, f32[4,16,1,256]{3,2,1,0:T(1,128)S(1)}, u32[]{:S(2)}, u32[]{:S(2)}) collective-permute-start(f32[4,16,1,256]{3,2,1,0:T(1,128)S(1)} %slice.606), channel_id=1, source_target_pairs={{2,0},{4,2},{6,4},{8,6},{10,8},{12,10},{14,12},{16,14},{18,16},{20... | collective-permute-start | bytes 196616 | tf_op jit(solution)/shard_map/ppermute | solution.py:12
  135.9 11.4 %collective-permute-start.28 = (f32[4,16,8,1]{3,2,1,0:T(8,128)S(1)}, f32[4,16,8,1]{3,2,1,0:T(8,128)S(1)}, u32[]{:S(2)}, u32[]{:S(2)}) collective-permute-start(f32[4,16,8,1]{3,2,1,0:T(8,128)S(1)} %slice.620), channel_id=1, source_target_pairs={{1,0},{3,2},{5,4},{7,6},{9,8},{11,10},{13,12},{15,14},{17,16},{19,... | collective-permute-start | bytes 6152 | tf_op jit(solution)/shard_map/ppermute | solution.py:12
  148.3 19.1 %collective-permute-start.29 = (f32[4,16,1,256]{3,2,1,0:T(1,128)S(1)}, f32[4,16,1,256]{3,2,1,0:T(1,128)S(1)}, u32[]{:S(2)}, u32[]{:S(2)}) collective-permute-start(f32[4,16,1,256]{3,2,1,0:T(1,128)S(1)} %slice.623), channel_id=1, source_target_pairs={{0,2},{2,4},{4,6},{6,8},{8,10},{10,12},{12,14},{14,16},{16,18},{18... | collective-permute-start | bytes 196616 | tf_op jit(solution)/shard_map/ppermute | solution.py:12
  150.2 21.0 %collective-permute-start.30 = (f32[4,16,1,256]{3,2,1,0:T(1,128)S(1)}, f32[4,16,1,256]{3,2,1,0:T(1,128)S(1)}, u32[]{:S(2)}, u32[]{:S(2)}) collective-permute-start(f32[4,16,1,256]{3,2,1,0:T(1,128)S(1)} %slice.625), channel_id=1, source_target_pairs={{0,2},{2,4},{4,6},{6,8},{8,10},{10,12},{12,14},{14,16},{16,18},{18... | collective-permute-start | bytes 196616 | tf_op jit(solution)/shard_map/ppermute | solution.py:12
  155.3 11.1 %collective-permute-start.24 = (f32[4,16,8,1]{3,2,1,0:T(8,128)S(1)}, f32[4,16,8,1]{3,2,1,0:T(8,128)S(1)}, u32[]{:S(2)}, u32[]{:S(2)}) collective-permute-start(f32[4,16,8,1]{3,2,1,0:T(8,128)S(1)} %slice.609), channel_id=1, source_target_pairs={{0,1},{2,3},{4,5},{6,7},{8,9},{10,11},{12,13},{14,15},{16,17},{18,... | collective-permute-start | bytes 6152 | tf_op jit(solution)/shard_map/ppermute | solution.py:12
  156.6 14.6 %collective-permute-start.31 = (f32[4,16,8,1]{3,2,1,0:T(8,128)S(1)}, f32[4,16,8,1]{3,2,1,0:T(8,128)S(1)}, u32[]{:S(2)}, u32[]{:S(2)}) collective-permute-start(f32[4,16,8,1]{3,2,1,0:T(8,128)S(1)} %slice.627), channel_id=1, source_target_pairs={{0,1},{2,3},{4,5},{6,7},{8,9},{10,11},{12,13},{14,15},{16,17},{18,... | collective-permute-start | bytes 6152 | tf_op jit(solution)/shard_map/ppermute | solution.py:12
  (20 other events, 196.5 us)
where the time goes:
time: 175 us; the launch traced here: 174 us
  starting transfers between devices  64.9 us (37%)
  waiting for transfers between devices  48.9 us (28%)
  other arithmetic  48.7 us (28%)
  local copies, waits for them, and re-layouts  9.38 us (5%)
  between operations  1.75 us (1%)
    ppermute x32, starting transfers between devices, from_behind(): lax.ppermute(value, axis, [(source, source + steps) for source in range(i...  64.9 us
    ppermute x32, waiting for transfers between devices, from_behind(): lax.ppermute(value, axis, [(source, source + steps) for source in range(i...  48.9 us
    mul x2, other arithmetic, run_steps(): state_v[pole] = [coef_b * state_u[pole][c] for c in range(3)]  10.3 us
    mul x2, other arithmetic, run_steps(): coef_a * state_u[pole][c] + state_v[pole][c] + coef_c * sectioned[c]  10.2 us
    select_n x2, other arithmetic, region_lookup(): value = jnp.where(region_ids == region, table[region, pole], value)  10.1 us
    add x9, other arithmetic, run_steps(): elec = [elec[c] + mask_float * residual[:, c] * scaled for c in range(3)]  5.31 us
    another operation x5, other arithmetic, run_steps(): return (jnp.stack(elec, 1), jnp.stack(magn, 1))  4.44 us
  transfers between devices with their start and end apart: 32, of which 12 were waited for; matrix products, arithmetic and copies ran while one was open for 26% of the time, Pallas kernels for 0%

commit v1 on v0

v1 whole, which is shorter than its diff:
```python
import functools

import jax
import jax.numpy as jnp
from jax import lax
from jax.experimental import pallas as pl
from jax.experimental.pallas import tpu as pltpu
from jax.sharding import PartitionSpec as P

LANES = 128
SUB = 8
HALF = LANES // 2
F32 = jnp.float32


def pairs(count, first):
    swaps = []
    for low in range(first, count - 1, 2):
        swaps += [(low, low + 1), (low + 1, low)]
    return swaps


def swap(value, axis, first):
    swaps = pairs(lax.axis_size(axis), first)
    return lax.ppermute(value, axis, swaps) if swaps else jnp.zeros_like(value)


def lane_index():
    return lax.broadcasted_iota(jnp.int32, (1, LANES), 1)


def pack_kernel(res, eps, ids, mask, near, far, strips):
    ports, comps, rows, _ = res.shape
    depth, items, tiles, nz, _ = near.shape
    nx = 2 * depth
    odd = lax.rem(lax.axis_index("gx"), 2)
    lane = lane_index()

    def plane(out, side, j, x):
        def rows_of(t):
            return pl.ds(t * nx + x, nz, stride=tiles * nx)

        masks = [mask[rows_of(t), :].astype(F32) for t in range(tiles)]
        strip = jnp.zeros((nz, LANES), F32)
        for k in range(items):
            vals = []
            for t in range(tiles):
                if k < ports * comps:
                    c, p = divmod(k, ports)
                    v = res[p, c, rows_of(t), :] * masks[t]
                elif k == ports * comps:
                    v = eps[rows_of(t), :]
                else:
                    v = ids[rows_of(t), :].astype(F32)
                out[j, k, t] = v
                vals.append(v)
            edge = jnp.where(lane < 4, vals[0], vals[-1])
            if k:
                edge = pltpu.roll(edge, 8 * k, 1)
            here = ((lane - 8 * k + 4) & (LANES - 1)) < 8
            strip = jnp.where(here, edge, strip)
        strips[side, j] = strip

    def body(j, carry):
        plane(near, 0, j, depth * (1 - odd) + j)
        plane(far, 1, j, depth * odd + j)
        return carry

    lax.fori_loop(0, depth, body, 0)


def solve_kernel(
    near, far, near_got, far_got, strips, strips_near, strips_far, pole_a, pole_b, pole_c, waveform, plan,
    out_e, out_h, elec, magn, hist, src, coef,
):
    depth, items, tiles, nz, _ = near.shape
    ports = waveform.shape[1]
    comps = 3
    regions = pole_a.shape[0]
    nx = 2 * depth
    gx = lax.axis_index("gx")
    gy = lax.axis_index("gy")
    odd = lax.rem(gx, 2)
    lane = lane_index()
    right, left = lane < 4, lane >= LANES - 4
    keep = jnp.where(right | (left & (gy > 0)), 1.0, 0.0).astype(F32)
    base = ports * comps
    amps = [[waveform[plan[s], p] for p in range(ports)] for s in range(depth)]

    gains = []
    for r in range(regions):
        total = [0.0] * depth
        for k in range(2):
            a, b, c = pole_a[r, k], pole_b[r, k], pole_c[r, k]
            before, now = 0.0, c
            for n in range(depth):
                total[n] = total[n] + (now - before)
                before, now = now, a * now + b * before
        gains.append(total)

    def set_coefs(x, t, eps_v, ids_v):
        vals = [jnp.zeros((nz, LANES), F32) for _ in range(depth)]
        for r in range(regions):
            here = ids_v == float(r)
            vals = [jnp.where(here, gains[r][n], vals[n]) for n in range(depth)]
        coef[x, 0, t] = 0.25 * eps_v
        coef[x, 1, t] = 1.0 - eps_v * vals[0]
        for n in range(1, depth):
            coef[x, 1 + n, t] = eps_v * vals[n]

    def take(source, strip, x, j):
        for k in range(items):
            vals = [source[j, k, t] for t in range(tiles)]
            s = strip(j)
            if k:
                s = pltpu.roll(s, LANES - 8 * k, 1)
            vals.append(jnp.where(right | left, s, 0.0))
            if k < base:
                c, p = divmod(k, ports)
                for t in range(tiles + 1):
                    src[x, p, c, t] = vals[t]
                    elec[x, p, c, t, pl.ds(0, nz), :] = amps[0][p] * vals[t]
                    elec[x, p, c, t, pl.ds(nz, SUB), :] = jnp.zeros((SUB, LANES), F32)
                    magn[x, p, c, t, pl.ds(0, SUB), :] = jnp.zeros((SUB, LANES), F32)
            elif k == base:
                eps_vals = vals
            else:
                for t in range(tiles + 1):
                    set_coefs(x, t, eps_vals[t], vals[t])

    def own(side):
        def load(j):
            return strips[side, j]

        return load

    def load_all(j, carry):
        take(near, own(0), depth + depth * (1 - odd) + j, j)
        take(far, own(1), depth + depth * odd + j, j)
        take(near_got, lambda j: strips_near[j], 3 * depth * (1 - odd) + j, j)
        take(far_got, lambda j: strips_far[j], 3 * depth * odd + j, j)
        return carry

    lax.fori_loop(0, depth, load_all, 0)

    def up_y(vals):
        rolled = [pltpu.roll(v, LANES - 1, 1) for v in vals]
        return [jnp.where(lane == LANES - 1, rolled[(t + 1) % (tiles + 1)], rolled[t]) for t in range(tiles + 1)]

    def down_y(vals):
        rolled = [pltpu.roll(v, 1, 1) for v in vals]
        return [jnp.where(lane == 0, rolled[(t - 1) % (tiles + 1)], rolled[t]) for t in range(tiles + 1)]

    everything = range(tiles + 1)

    def step_h(s, x):
        for p in range(ports):
            for z in range(0, nz, SUB):
                def e(c, dx=0, dz=0):
                    return [elec[x + dx, p, c, t, pl.ds(z + dz, SUB), :] for t in everything]

                ex, ey, ez = e(0), e(1), e(2)
                ex_z, ey_z = e(0, 0, 1), e(1, 0, 1)
                ey_x, ez_x = e(1, 1), e(2, 1)
                ex_y, ez_y = up_y(ex), up_y(ez)
                for t in everything:
                    curls = (
                        (ez_y[t] - ez[t]) - (ey_z[t] - ey[t]),
                        (ex_z[t] - ex[t]) - (ez_x[t] - ez[t]),
                        (ey_x[t] - ey[t]) - (ex_y[t] - ex[t]),
                    )
                    for c in range(comps):
                        where = (x, p, c, t, pl.ds(SUB + z, SUB), slice(None))
                        new = -curls[c] if s == 0 else magn[where] - curls[c]
                        magn[where] = new * keep if t == tiles else new

    def step_e(s, x):
        for p in range(ports):
            for z in range(0, nz, SUB):
                def h(c, dx=0, dz=0):
                    return [magn[x + dx, p, c, t, pl.ds(SUB + z + dz, SUB), :] for t in everything]

                hx, hy, hz = h(0), h(1), h(2)
                hx_z, hy_z = h(0, 0, -1), h(1, 0, -1)
                hy_x, hz_x = h(1, -1), h(2, -1)
                hx_y, hz_y = down_y(hx), down_y(hz)
                rows = pl.ds(z, SUB)
                for t in everything:
                    if s == depth - 1 and t == tiles:
                        continue
                    w = [coef[x, n, t, rows, :] for n in range(s + 2)]
                    curls = (
                        (hz[t] - hz_y[t]) - (hy[t] - hy_z[t]),
                        (hx[t] - hx_z[t]) - (hz[t] - hz_x[t]),
                        (hy[t] - hy_x[t]) - (hx[t] - hx_y[t]),
                    )
                    mags = (hx, hy, hz)
                    for c in range(comps):
                        sec = elec[x, p, c, t, rows, :] + w[0] * curls[c]
                        new = w[1] * sec
                        for n in range(1, s + 1):
                            new = new - w[1 + n] * hist[s - n, x, p, c, t, rows, :]
                        if s < depth - 1:
                            hist[s, x, p, c, t, rows, :] = sec
                            elec[x, p, c, t, rows, :] = new + amps[s + 1][p] * src[x, p, c, t, rows, :]
                        else:
                            out = pl.ds(z * tiles * nx + t * nx + (x - depth), SUB, stride=tiles * nx)
                            out_e[p, c, out, :] = new
                            out_h[p, c, out, :] = 0.5 * mags[c][t]

    first = gx == 0

    @pl.when(first)
    def _():
        magn[depth - 1] = jnp.zeros(magn.shape[1:], F32)

    last = 4 * depth - 2
    for s in range(depth):
        low = jnp.where(first, depth, s)
        pl.loop(low, last - s + 1)(functools.partial(step_h, s))
        pl.loop(jnp.where(first, depth, s + 1), last - s + 1)(functools.partial(step_e, s))


def local(residual, eps_inv, region_ids, source_mask, pole_a, pole_b, pole_c, waveform, plan):
    ports, comps, nz, nx, ny = residual.shape
    depth = plan.shape[0]
    tiles = ny // LANES
    assert nx == 2 * depth and ny % LANES == 0 and nx == SUB
    items = ports * comps + 2

    def tiled(v):
        lead = v.shape[:-2]
        v = v.reshape(lead + (nx, tiles, LANES))
        v = jnp.swapaxes(v, -3, -2)
        return v.reshape(lead[:-1] + (nz * tiles * nx, LANES))

    def untiled(v):
        v = v.reshape(v.shape[:-2] + (nz, tiles, nx, LANES))
        v = jnp.swapaxes(v, -3, -2)
        return v.reshape(v.shape[:-2] + (ny,))

    vmem = pl.BlockSpec(memory_space=pltpu.VMEM)
    smem = pl.BlockSpec(memory_space=pltpu.SMEM)
    half = jax.ShapeDtypeStruct((depth, items, tiles, nz, LANES), F32)
    near, far, edges = pl.pallas_call(
        pack_kernel,
        out_shape=(half, half, jax.ShapeDtypeStruct((2, depth, nz, LANES), F32)),
        in_specs=[vmem] * 4,
        out_specs=(vmem,) * 3,
        name="pack",
    )(tiled(residual), tiled(eps_inv), tiled(region_ids), tiled(source_mask))

    far_got = swap(far, "gx", 1)
    near_got = swap(near, "gx", 0)
    one, two = swap(edges, "gy", 0), swap(edges, "gy", 1)
    odd_y = lax.rem(lax.axis_index("gy"), 2) == 1
    lane = lane_index()
    if lax.axis_size("gy") > 2:
        above, below = jnp.where(odd_y, two, one), jnp.where(odd_y, one, two)
    else:
        above, below = jnp.where(odd_y, 0.0, one), jnp.where(odd_y, one, 0.0)
    strips = jnp.where((lane & 7) < 4, above, below)
    strips_near = swap(strips[0], "gx", 0)
    strips_far = swap(strips[1], "gx", 1)

    out = jax.ShapeDtypeStruct((ports, comps, nz * tiles * nx, LANES), F32)
    planes = 2 * nx
    field = (planes, ports, comps, tiles + 1)
    out_e, out_h = pl.pallas_call(
        solve_kernel,
        out_shape=(out, out),
        in_specs=[vmem] * 7 + [smem] * 5,
        out_specs=(vmem, vmem),
        scratch_shapes=[
            pltpu.VMEM(field + (nz + SUB, LANES), F32),
            pltpu.VMEM(field + (nz + SUB, LANES), F32),
            pltpu.VMEM((depth - 1,) + field + (nz, LANES), F32),
            pltpu.VMEM(field + (nz, LANES), F32),
            pltpu.VMEM((planes, 1 + depth, tiles + 1, nz, LANES), F32),
        ],
        compiler_params=pltpu.CompilerParams(vmem_limit_bytes=56 << 20),
        name="solve",
    )(near, far, near_got, far_got, strips, strips_near, strips_far, pole_a, pole_b, pole_c, waveform, plan)
    return untiled(out_e), untiled(out_h)


def solution(mesh):
    placed = (
        P(None, None, None, "gx", "gy"),
        P(None, "gx", "gy"),
        P(None, "gx", "gy"),
        P(None, "gx", "gy"),
        P(),
        P(),
        P(),
        P(),
        P(),
    )
    return jax.shard_map(
        local,
        mesh=mesh,
        in_specs=placed,
        out_specs=(P(None, None, None, "gx", "gy"), P(None, None, None, "gx", "gy")),
        check_vma=False,
    )
```

time: 175 us -> 50.9 us (0.29)
  starting transfers between devices: 64.9 us -> 6.44 us
  other arithmetic: 48.7 us -> 0.02 us
  waiting for transfers between devices: 48.9 us -> 16.2 us
  Pallas kernels: 0 us -> 22 us
  local copies, waits for them, and re-layouts: 9.38 us -> 4.6 us
    ppermute x32 -> x5, starting transfers between devices: 64.9 us -> 6.44 us  [swap(): return lax.ppermute(value, axis, swaps) if swaps else jnp.zeros_like(value)]
    ppermute x32 -> x5, waiting for transfers between devices: 48.9 us -> 16.2 us  [swap(): return lax.ppermute(value, axis, swaps) if swaps else jnp.zeros_like(value)]
    mul x5 -> x0, other arithmetic: 22.2 us -> none  [the longest x2 10.3 us: run_steps(): state_v[pole] = [coef_b * state_u[pole][c] for c in range(3)]]
    pallas_call x0 -> x2, Pallas kernels: none -> 22 us  [the longest x1 18.4 us: local(): pl.pallas_call(solve_kernel, out_shape=(out, out), in_specs=[vmem] * 7 +...]
    select_n x2 -> x1, other arithmetic: 10.1 us -> 0.01 us  [local(): strips = jnp.where(lane & 7 < 4, above, below)]
    slice x70 -> x0, local copies, waits for them, and re-layouts: 7.99 us -> none  [the longest x3 2.15 us: region_lookup(): value = jnp.where(region_ids == region, table[region, pole], value)]
    add x9 -> x0, other arithmetic: 5.31 us -> none  [run_steps(): elec = [elec[c] + mask_float * residual[:, c] * scaled for c in range(3)]]
    another operation x5 -> x0, other arithmetic: 4.44 us -> none  [run_steps(): return (jnp.stack(elec, 1), jnp.stack(magn, 1))]
  transfers between devices with their start and end apart: 32 -> 5, of which waited for: 12 -> 2; matrix products, arithmetic and copies ran while one was open for 26% -> 5% of each run, Pallas kernels for 0% -> 0%
where the time goes in v1:
time: 50.9 us; the launch traced here: 50 us
  Pallas kernels  22 us (43%)
  waiting for transfers between devices  16.2 us (32%)
  starting transfers between devices  6.44 us (13%)
  local copies, waits for them, and re-layouts  4.6 us (9%)
  between operations  0.76 us (1%)
    pallas_call x1, Pallas kernels, local(): pl.pallas_call(solve_kernel, out_shape=(out, out), in_specs=[vmem] * 7 +...  18.4 us
    ppermute x5, waiting for transfers between devices, swap(): return lax.ppermute(value, axis, swaps) if swaps else jnp.zeros_like(value)  16.2 us
    ppermute x5, starting transfers between devices, swap(): return lax.ppermute(value, axis, swaps) if swaps else jnp.zeros_like(value)  6.44 us
    unnamed x22, local copies, waits for them, and re-layouts  4.6 us
    pallas_call x1, Pallas kernels, local(): pl.pallas_call(pack_kernel, out_shape=(half, half, jax.ShapeDtypeStruct((...  3.59 us
  transfers between devices with their start and end apart: 5, of which 2 were waited for; matrix products, arithmetic and copies ran while one was open for 5% of the time, Pallas kernels for 0%

profile of v1, /device:TPU:6, one launch (start us, length us, event | category | flops | bytes accessed | tf_op | source)
XLA Modules:
  0.0 50.0 jit_solution(2726482292174582420)
XLA Ops:
  0.6 0.0 copy-start.6
  0.6 0.0 copy-start.7
  0.7 3.6 %pack.1 = (f32[4,14,2,16,128]{4,3,2,1,0:T(8,128)}, f32[4,14,2,16,128]{4,3,2,1,0:T(8,128)}, f32[2,4,16,128]{3,2,1,0:T(8,128)}) custom-call(f32[4,3,256,128]{3,2,1,0:T(8,128)} %bitcast.34, f32[256,128]{1,0:T(8,128)} %bitcast.35, s32[256,128]{1,0:T(8,128)} %bitcast.36, s32[256,128]{1,0:T(8,128)} %bitcast.37), custom_call_target="tpu_custom_call" | custom-call | tf_op jit(solution)/shard_map/pack/pallas_call | solution.py:245
  4.3 0.0 collective-permute-start
  4.3 2.5 %collective-permute-start.1 = (f32[4,14,2,16,128]{4,3,2,1,0:T(8,128)}, f32[4,14,2,16,128]{4,3,2,1,0:T(8,128)S(1)}, u32[]{:S(2)}, u32[]{:S(2)}) collective-permute-start(f32[4,14,2,16,128]{4,3,2,1,0:T(8,128)} %get-tuple-element.8.far), channel_id=1, source_target_pairs={{2,4},{4,2},{6,8},{8,6},{10,12},{12,10},{14,16},{16,14},{18,20},{2... | collective-permute-start | bytes 2752520 | tf_op jit(solution)/shard_map/ppermute | solution.py:25
  6.8 0.1 collective-permute-start.2
  6.9 5.1 %collective-permute-done.2 = f32[2,4,16,128]{3,2,1,0:T(8,128)S(1)} collective-permute-done((f32[2,4,16,128]{3,2,1,0:T(8,128)}, f32[2,4,16,128]{3,2,1,0:T(8,128)S(1)}, u32[]{:S(2)}, u32[]{:S(2)}) %collective-permute-start.2) | collective-permute-done | bytes 65568 | tf_op jit(solution)/shard_map/ppermute | solution.py:25
  12.1 1.9 %collective-permute-start.4 = (f32[4,16,128]{2,1,0:T(8,128)S(1)}, f32[4,16,128]{2,1,0:T(8,128)S(1)}, u32[]{:S(2)}, u32[]{:S(2)}) collective-permute-start(f32[4,16,128]{2,1,0:T(8,128)S(1)} %get-tuple-element.12), channel_id=1, source_target_pairs={{2,4},{4,2},{6,8},{8,6},{10,12},{12,10},{14,16},{16,14},{18,20},{2... | collective-permute-start | bytes 98312 | tf_op jit(solution)/shard_map/ppermute | solution.py:25
  14.0 1.9 %collective-permute-start.3 = (f32[4,16,128]{2,1,0:T(8,128)S(1)}, f32[4,16,128]{2,1,0:T(8,128)S(1)}, u32[]{:S(2)}, u32[]{:S(2)}) collective-permute-start(f32[4,16,128]{2,1,0:T(8,128)S(1)} %get-tuple-element.13), channel_id=1, source_target_pairs={{0,2},{2,0},{4,6},{6,4},{8,10},{10,8},{12,14},{14,12},{16,18},{18,... | collective-permute-start | bytes 98312 | tf_op jit(solution)/shard_map/ppermute | solution.py:25
  15.9 0.0 copy-done.6
  15.9 0.7 %copy.11.pole_a = f32[8,2]{1,0:T(8,128)} copy(f32[8,2]{0,1:T(2,128)S(1)} %copy-done.6) | data formatting | bytes 128 | tf_op args[4]
  16.6 0.7 %copy.12.pole_b = f32[8,2]{1,0:T(8,128)} copy(f32[8,2]{0,1:T(2,128)S(1)} %copy-done.7) | data formatting | bytes 128 | tf_op args[5]
  17.2 0.0 copy-done.8
  17.2 0.7 %copy.13.pole_c = f32[8,2]{1,0:T(8,128)} copy(f32[8,2]{0,1:T(2,128)S(1)} %copy-done.8) | data formatting | bytes 128 | tf_op args[6]
  17.9 0.7 %copy.14.waveform = f32[64,4]{1,0:T(8,128)} copy(f32[64,4]{0,1:T(4,128)S(1)} %copy-done.5) | data formatting | bytes 2048 | tf_op args[7]
  18.6 11.1 %collective-permute-done.4.strips_far = f32[4,16,128]{2,1,0:T(8,128)S(1)} collective-permute-done((f32[4,16,128]{2,1,0:T(8,128)S(1)}, f32[4,16,128]{2,1,0:T(8,128)S(1)}, u32[]{:S(2)}, u32[]{:S(2)}) %collective-permute-start.4) | collective-permute-done | bytes 32800 | tf_op jit(solution)/shard_map/ppermute | solution.py:25
  29.7 0.0 collective-permute-done.3.strips_near
  29.7 0.0 collective-permute-done.near_got
  29.7 0.0 collective-permute-done.1.far_got
  29.8 0.6 %copy-done.3 = f32[4,16,128]{2,1,0:T(8,128)} copy-done((f32[4,16,128]{2,1,0:T(8,128)}, f32[4,16,128]{2,1,0:T(8,128)S(1)}, u32[]{:S(2)}) %copy-start.3) | copy-done | bytes 32792
  30.3 0.0 copy-done.4
  30.3 0.3 copy-done
  30.7 0.9 %copy-done.1 = f32[4,14,2,16,128]{4,3,2,1,0:T(8,128)} copy-done((f32[4,14,2,16,128]{4,3,2,1,0:T(8,128)}, f32[4,14,2,16,128]{4,3,2,1,0:T(8,128)S(1)}, u32[]{:S(2)}) %copy-start.1) | copy-done | bytes 917528
  31.6 18.4 %solve.1 = (f32[4,3,256,128]{3,2,1,0:T(8,128)}, f32[4,3,256,128]{3,2,1,0:T(8,128)}) custom-call(f32[4,14,2,16,128]{4,3,2,1,0:T(8,128)} %get-tuple-element.7.near, f32[4,14,2,16,128]{4,3,2,1,0:T(8,128)} %get-tuple-element.8.far, f32[4,14,2,16,128]{4,3,2,1,0:T(8,128)} %copy-done, f32[4,14,2,16,128]{4,3,2,1,0:T(8,128)} %copy-done.1, ...), custom_call_target="tpu_custom_call" | custom-call | tf_op jit(solution)/shard_map/solve/pallas_call | solution.py:269
  (13 shorter events, 0.0 us)
Async XLA Ops:
  0.6 15.3 %copy-start.6 = (f32[8,2]{0,1:T(2,128)S(1)}, f32[8,2]{0,1:T(2,128)}, u32[]{:S(2)}) copy-start(f32[8,2]{0,1:T(2,128)} %param.13) | copy-start | bytes 196
  0.6 15.9 %copy-start.7 = (f32[8,2]{0,1:T(2,128)S(1)}, f32[8,2]{0,1:T(2,128)}, u32[]{:S(2)}) copy-start(f32[8,2]{0,1:T(2,128)} %param.14) | copy-start | bytes 196
  0.7 16.6 %copy-start.8 = (f32[8,2]{0,1:T(2,128)S(1)}, f32[8,2]{0,1:T(2,128)}, u32[]{:S(2)}) copy-start(f32[8,2]{0,1:T(2,128)} %param.15) | copy-start | bytes 196
  0.7 17.2 %copy-start.5 = (f32[64,4]{0,1:T(4,128)S(1)}, f32[64,4]{0,1:T(4,128)}, u32[]{:S(2)}) copy-start(f32[64,4]{0,1:T(4,128)} %param.16) | copy-start | bytes 3076
  4.3 25.5 %collective-permute-start = (f32[4,14,2,16,128]{4,3,2,1,0:T(8,128)}, f32[4,14,2,16,128]{4,3,2,1,0:T(8,128)S(1)}, u32[]{:S(2)}, u32[]{:S(2)}) collective-permute-start(f32[4,14,2,16,128]{4,3,2,1,0:T(8,128)} %get-tuple-element.7.near), channel_id=1, source_target_pairs={{0,2},{2,0},{4,6},{6,4},{8,10},{10,8},{12,14},{14,12},{16,18},{18,... | collective-permute-start | bytes 2752520 | tf_op jit(solution)/shard_map/ppermute | solution.py:25
  4.3 25.5 %collective-permute-start.1 = (f32[4,14,2,16,128]{4,3,2,1,0:T(8,128)}, f32[4,14,2,16,128]{4,3,2,1,0:T(8,128)S(1)}, u32[]{:S(2)}, u32[]{:S(2)}) collective-permute-start(f32[4,14,2,16,128]{4,3,2,1,0:T(8,128)} %get-tuple-element.8.far), channel_id=1, source_target_pairs={{2,4},{4,2},{6,8},{8,6},{10,12},{12,10},{14,16},{16,14},{18,20},{2... | collective-permute-start | bytes 2752520 | tf_op jit(solution)/shard_map/ppermute | solution.py:25
  6.8 5.2 %collective-permute-start.2 = (f32[2,4,16,128]{3,2,1,0:T(8,128)}, f32[2,4,16,128]{3,2,1,0:T(8,128)S(1)}, u32[]{:S(2)}, u32[]{:S(2)}) collective-permute-start(f32[2,4,16,128]{3,2,1,0:T(8,128)} %get-tuple-element.9), channel_id=1, source_target_pairs={{0,1},{1,0},{2,3},{3,2},{4,5},{5,4},{6,7},{7,6},{8,9},{9,8},{10,11... | collective-permute-start | bytes 196616 | tf_op jit(solution)/shard_map/ppermute | solution.py:25
  12.0 17.7 %copy-start.2 = (f32[2,4,16,128]{3,2,1,0:T(8,128)}, f32[2,4,16,128]{3,2,1,0:T(8,128)S(1)}, u32[]{:S(2)}) copy-start(f32[2,4,16,128]{3,2,1,0:T(8,128)S(1)} %select_select_fusion.strips) | copy-start | bytes 196612
  12.1 17.7 %collective-permute-start.4 = (f32[4,16,128]{2,1,0:T(8,128)S(1)}, f32[4,16,128]{2,1,0:T(8,128)S(1)}, u32[]{:S(2)}, u32[]{:S(2)}) collective-permute-start(f32[4,16,128]{2,1,0:T(8,128)S(1)} %get-tuple-element.12), channel_id=1, source_target_pairs={{2,4},{4,2},{6,8},{8,6},{10,12},{12,10},{14,16},{16,14},{18,20},{2... | collective-permute-start | bytes 98312 | tf_op jit(solution)/shard_map/ppermute | solution.py:25
  14.0 15.7 %collective-permute-start.3 = (f32[4,16,128]{2,1,0:T(8,128)S(1)}, f32[4,16,128]{2,1,0:T(8,128)S(1)}, u32[]{:S(2)}, u32[]{:S(2)}) collective-permute-start(f32[4,16,128]{2,1,0:T(8,128)S(1)} %get-tuple-element.13), channel_id=1, source_target_pairs={{0,2},{2,0},{4,6},{6,4},{8,10},{10,8},{12,14},{14,12},{16,18},{18,... | collective-permute-start | bytes 98312 | tf_op jit(solution)/shard_map/ppermute | solution.py:25
  29.7 0.6 %copy-start.3 = (f32[4,16,128]{2,1,0:T(8,128)}, f32[4,16,128]{2,1,0:T(8,128)S(1)}, u32[]{:S(2)}) copy-start(f32[4,16,128]{2,1,0:T(8,128)S(1)} %collective-permute-done.4.strips_far) | copy-start | bytes 98308
  29.7 0.6 %copy-start.4 = (f32[4,16,128]{2,1,0:T(8,128)}, f32[4,16,128]{2,1,0:T(8,128)S(1)}, u32[]{:S(2)}) copy-start(f32[4,16,128]{2,1,0:T(8,128)S(1)} %collective-permute-done.3.strips_near) | copy-start | bytes 98308
  29.7 0.9 %copy-start = (f32[4,14,2,16,128]{4,3,2,1,0:T(8,128)}, f32[4,14,2,16,128]{4,3,2,1,0:T(8,128)S(1)}, u32[]{:S(2)}) copy-start(f32[4,14,2,16,128]{4,3,2,1,0:T(8,128)S(1)} %collective-permute-done.near_got) | copy-start | bytes 2752516
  30.7 0.9 %copy-start.1 = (f32[4,14,2,16,128]{4,3,2,1,0:T(8,128)}, f32[4,14,2,16,128]{4,3,2,1,0:T(8,128)S(1)}, u32[]{:S(2)}) copy-start(f32[4,14,2,16,128]{4,3,2,1,0:T(8,128)S(1)} %collective-permute-done.1.far_got) | copy-start | bytes 2752516
